TPU v7x, 32 devices: a whole 2x2x4 slice. The times are simulated.
32 devices in a mesh: dp: 8 (over z, y), row: 2 (over x), col: 2 (over core).
Axes of the slice: x: 2, y: 2, z: 4, core: 2. Of those that a mesh axis runs over, the one named last changes fastest.
Arguments:
- tokens: bfloat16 [12288, 1024], P('dp', 'row'), may hold values from -6 to 6
- gain_attn: float32 [1024], replicated, may hold values from 0.5 to 1.5
- w_qkv: float32 [1024, 16, 192], P('row', 'col'), may hold values from -0.1875 to 0.1875
- w_out: float32 [1024, 1024], P('col', 'row'), may hold values from -3 to 3
- gain_mlp: float32 [1024], replicated, may hold values from 0.5 to 1.5
- w_in: float32 [1024, 2, 2624], P('row', None, 'col'), may hold values from -0.1875 to 0.1875
- w_down: float32 [2624, 1024], P('col', 'row'), may hold values from -0.125 to 0.125
- cotangent: bfloat16 [12288, 1024], P('dp', 'row'), may hold values from -6 to 6
- seq_lengths: int32 [16], replicated, may hold values from 256 to 1024, as said below
- seq_offsets: int32 [16], replicated, may hold values from 0 to 11264, as said below
- deal: int32 [16], replicated, may hold values from 0 to 15, as said below
Outputs:
- layer_out: bfloat16 [12288, 1024], P('dp', 'row')
- tokens_grad: bfloat16 [12288, 1024], P('dp', 'row')
- gain_attn_grad: float32 [1024], P(('dp', 'row'))
- w_qkv_grad: float32 [1024, 16, 192], P(('dp', 'row'), 'col')
- w_out_grad: float32 [1024, 1024], P('col', ('dp', 'row'))
- gain_mlp_grad: float32 [1024], P(('dp', 'row'))
- w_in_grad: float32 [1024, 2, 2624], P(('dp', 'row'), None, 'col')
- w_down_grad: float32 [2624, 1024], P('col', ('dp', 'row'))
Inputs may be any that keep to these rules, and one draw needn't show every extreme that they name: `seq_lengths`: each group holds one sequence of 1024 tokens, its others have at most half of 1024, and some group fills all 1536 slots. Sequence 16 - 1 has 1024 tokens. Sequences 0 to 14 lie end to end in index order from place 0: seq_offsets[s] is the sum of the lengths of sequences 0 to s - 1. Sequence 16 - 1 ends at the last token place; places between belong to no sequence. `deal`: A permutation of the 16 sequences.
All inputs are finite; a program needn't handle non-finite values.
Results may differ from a plain program's by a relative error of at most 0.017.
Values may be sent and summed in bfloat16 or wider, within the bound.
No kernel may reach another device: no remote copies, remote signals or barrier semaphores. Data moves between devices by JAX's collectives and lax.ppermute only.
A program may use at most 192 MiB of HBM per device.

v0:
```python
import math
import jax
import jax.numpy as jnp
from jax import lax
from jax.sharding import PartitionSpec as P

SEQ_GRP = 2
CAP = 1536
epsilon = 1e-05
rope_base = 160000.0


def slot_table(seq_lengths, seq_offsets, deal, group_index):
    members = lax.dynamic_slice_in_dim(deal, group_index * SEQ_GRP, SEQ_GRP)
    every = jnp.arange(deal.shape[0], dtype=jnp.int32)
    matches = every[None, :] == members[:, None]
    member_lengths = jnp.sum(jnp.where(matches, seq_lengths[None, :], 0), axis=1)
    member_offsets = jnp.sum(jnp.where(matches, seq_offsets[None, :], 0), axis=1)
    member_starts = jnp.cumsum(member_lengths) - member_lengths
    slots = jnp.arange(CAP, dtype=jnp.int32)
    inside = (slots[:, None] >= member_starts[None, :]) & (
        slots[:, None] < (member_starts + member_lengths)[None, :]
    )
    live = jnp.any(inside, axis=1)
    places = slots - jnp.sum(jnp.where(inside, member_starts[None, :], 0), axis=1)
    segment = jnp.sum(
        jnp.where(inside, jnp.arange(SEQ_GRP, dtype=jnp.int32)[None, :], 0), axis=1
    ) + jnp.where(live, 0, SEQ_GRP)
    source = jnp.where(
        live, jnp.sum(jnp.where(inside, member_offsets[None, :], 0), axis=1) + places, -1
    )
    return (source, places, segment)


def home_slots(seq_lengths, seq_offsets, deal, group_index, block_length):
    every = jnp.arange(deal.shape[0], dtype=jnp.int32)
    dealt = deal[None, :] == every[:, None]
    place_of = jnp.sum(jnp.where(dealt, every[None, :], 0), axis=1)
    dealt_lengths = jnp.sum(jnp.where(dealt, seq_lengths[:, None], 0), axis=0)
    grouped = dealt_lengths.reshape(-1, SEQ_GRP)
    place_starts = (jnp.cumsum(grouped, axis=1) - grouped).reshape(-1)
    slot_starts = jnp.sum(jnp.where(dealt, place_starts[None, :], 0), axis=1)
    homes = place_of // SEQ_GRP * CAP + slot_starts - seq_offsets
    given = group_index * block_length + jnp.arange(block_length, dtype=jnp.int32)
    inside = (given[:, None] >= seq_offsets[None, :]) & (
        given[:, None] < (seq_offsets + seq_lengths)[None, :]
    )
    target = jnp.where(
        jnp.any(inside, axis=1), jnp.sum(jnp.where(inside, homes[None, :], 0), axis=1) + given, -1
    )
    return target


def take_rows(kept, incoming, relative):
    row_count = incoming[0].shape[0]
    usable = ((relative >= 0) & (relative < row_count))[:, None]
    picked = jnp.clip(relative, 0, row_count - 1)
    return tuple(
        (
            jnp.where(usable, jnp.take(arriving, picked, axis=0), holding)
            for holding, arriving in zip(kept, incoming)
        )
    )


def rope_tables(places, head_width):
    freq = rope_base ** (-(jnp.arange(0, head_width, 2, dtype=jnp.float32) / head_width))
    angle = places.astype(jnp.float32)[:, None, None] * freq[None, None, :]
    return (jnp.cos(angle), jnp.sin(angle))


def turn(part, cosine, sine):
    half = part.shape[-1] // 2
    first_half = part[..., :half]
    second_half = part[..., half:]
    return jnp.concatenate(
        [first_half * cosine - second_half * sine, second_half * cosine + first_half * sine],
        axis=-1,
    )


def turn_back(grad, cosine, sine):
    half = grad.shape[-1] // 2
    first_half = grad[..., :half]
    second_half = grad[..., half:]
    return jnp.concatenate(
        [first_half * cosine + second_half * sine, second_half * cosine - first_half * sine],
        axis=-1,
    )


def norm_forward(value, gain):
    center = value - jnp.mean(value, axis=-1, keepdims=True)
    inverse = lax.rsqrt(jnp.mean(center * center, axis=-1, keepdims=True) + epsilon)
    normed = center * inverse
    return (normed * gain, normed, inverse)


def norm_backward(grad, gain, normed, inverse):
    scaled = grad * gain
    back = inverse * (
        scaled
        - jnp.mean(scaled, axis=-1, keepdims=True)
        - normed * jnp.mean(scaled * normed, axis=-1, keepdims=True)
    )
    return (back, jnp.sum(grad * normed, axis=0))


def geglu(first_part, second_part):
    return jax.nn.gelu(first_part, approximate=False) * second_part


def attend(by_head, segment):
    capacity, head_count, triple_width = by_head.shape
    head_width = triple_width // 3
    block_rows = min(512, capacity)
    block_count = capacity // block_rows
    keys = by_head[:, :, head_width : 2 * head_width]
    values = by_head[:, :, 2 * head_width :]
    factor = 1.0 / math.sqrt(head_width)

    def one_block(position):
        first = position * block_rows
        query = lax.dynamic_slice_in_dim(by_head, first, block_rows, 0)[:, :, :head_width]
        query_seg = lax.dynamic_slice_in_dim(segment, first, block_rows, 0)
        scores = (
            jnp.einsum("qhd,khd->hqk", query, keys, preferred_element_type=jnp.float32) * factor
        )
        same_seq = (query_seg[:, None] == segment[None, :])[None]
        scores = jnp.where(same_seq, scores, -1e30)
        top_score = jnp.max(scores, axis=-1, keepdims=True)
        raised = jnp.exp(scores - top_score)
        denominator = jnp.sum(raised, axis=-1, keepdims=True)
        probs = (raised / denominator).astype(jnp.bfloat16)
        attended = jnp.einsum(
            "hqk,khd->qhd", probs, values, preferred_element_type=jnp.float32
        ).astype(jnp.bfloat16)
        return (attended, (top_score + jnp.log(denominator))[..., 0])

    attended, log_totals = lax.map(one_block, jnp.arange(block_count, dtype=jnp.int32))
    return (attended.reshape(capacity, head_count, head_width), log_totals)


def attend_back(by_head, grad_out, log_totals, segment):
    capacity, head_count, triple_width = by_head.shape
    head_width = triple_width // 3
    block_rows = min(512, capacity)
    block_count = capacity // block_rows
    keys = by_head[:, :, head_width : 2 * head_width]
    values = by_head[:, :, 2 * head_width :]
    factor = 1.0 / math.sqrt(head_width)

    def one_block(sums, position):
        key_grads, value_grads = sums
        first = position * block_rows
        query = lax.dynamic_slice_in_dim(by_head, first, block_rows, 0)[:, :, :head_width]
        query_seg = lax.dynamic_slice_in_dim(segment, first, block_rows, 0)
        grad_rows = lax.dynamic_slice_in_dim(grad_out, first, block_rows, 0)
        scores = (
            jnp.einsum("qhd,khd->hqk", query, keys, preferred_element_type=jnp.float32) * factor
        )
        same_seq = (query_seg[:, None] == segment[None, :])[None]
        probs = jnp.where(same_seq, jnp.exp(scores - log_totals[position][:, :, None]), 0.0)
        grad_probs = jnp.einsum(
            "qhd,khd->hqk", grad_rows, values, preferred_element_type=jnp.float32
        )
        value_grads = value_grads + jnp.einsum(
            "hqk,qhd->khd",
            probs.astype(jnp.bfloat16),
            grad_rows,
            preferred_element_type=jnp.float32,
        )
        centered = jnp.sum(probs * grad_probs, axis=-1, keepdims=True)
        grad_scores = (probs * (grad_probs - centered)).astype(jnp.bfloat16)
        query_grads = (
            jnp.einsum("hqk,khd->qhd", grad_scores, keys, preferred_element_type=jnp.float32)
            * factor
        )
        key_grads = (
            key_grads
            + jnp.einsum("hqk,qhd->khd", grad_scores, query, preferred_element_type=jnp.float32)
            * factor
        )
        return ((key_grads, value_grads), query_grads)

    empty = jnp.zeros((capacity, head_count, head_width), jnp.float32)
    (key_grads, value_grads), query_grads = lax.scan(
        one_block, (empty, empty), jnp.arange(block_count, dtype=jnp.int32)
    )
    return (query_grads.reshape(capacity, head_count, head_width), key_grads, value_grads)


def local(
    tokens,
    gain_attn,
    w_qkv,
    w_out,
    gain_mlp,
    w_in,
    w_down,
    cotangent,
    seq_lengths,
    seq_offsets,
    deal,
):
    group_index = lax.axis_index("dp")
    row_index = lax.axis_index("row")
    row_count = CAP // lax.axis_size("row")
    source, places, segment = slot_table(seq_lengths, seq_offsets, deal, group_index)
    blank = jnp.zeros((CAP, tokens.shape[1]), jnp.bfloat16)
    group_in, group_grad = take_rows(
        (blank, blank),
        (
            lax.all_gather(tokens, "dp", axis=0, tiled=True),
            lax.all_gather(cotangent, "dp", axis=0, tiled=True),
        ),
        source,
    )
    w_query, w_proj, w_gate, w_lower = (
        lax.all_gather(w_qkv.astype(jnp.bfloat16), "row", axis=0, tiled=True),
        lax.all_gather(w_out.astype(jnp.bfloat16), "row", axis=1, tiled=True),
        lax.all_gather(w_in.astype(jnp.bfloat16), "row", axis=0, tiled=True),
        lax.all_gather(w_down.astype(jnp.bfloat16), "row", axis=1, tiled=True),
    )
    rows_in, rows_grad = (
        lax.all_to_all(group_in, "row", split_axis=0, concat_axis=1, tiled=True),
        lax.all_to_all(group_grad, "row", split_axis=0, concat_axis=1, tiled=True),
    )
    head_width = w_query.shape[2] // 3
    my_places = lax.dynamic_slice_in_dim(places, row_index * row_count, row_count)
    cosine, sine = rope_tables(my_places, head_width)
    resid = rows_in.astype(jnp.float32)
    normed_one, unit_one, inverse_one = norm_forward(resid, gain_attn)
    normed_one = normed_one.astype(jnp.bfloat16)
    triples = jnp.einsum("td,dhe->the", normed_one, w_query, preferred_element_type=jnp.float32)
    turned = jnp.concatenate(
        [
            turn(triples[..., :head_width], cosine, sine),
            turn(triples[..., head_width : 2 * head_width], cosine, sine),
            triples[..., 2 * head_width :],
        ],
        axis=-1,
    ).astype(jnp.bfloat16)
    by_head = lax.all_to_all(turned, "row", split_axis=1, concat_axis=0, tiled=True)
    attended, log_totals = attend(by_head, segment)
    attn_rows = lax.all_to_all(attended, "row", split_axis=0, concat_axis=1, tiled=True)
    attn_flat = attn_rows.reshape(row_count, -1)
    mixed = resid + lax.psum(jnp.dot(attn_flat, w_proj, preferred_element_type=jnp.float32), "col")
    normed_two, unit_two, inverse_two = norm_forward(mixed, gain_mlp)
    normed_two = normed_two.astype(jnp.bfloat16)
    both = jnp.einsum("td,dgf->tgf", normed_two, w_gate, preferred_element_type=jnp.float32)
    hidden_f32, geglu_back = jax.vjp(geglu, both[:, 0], both[:, 1])
    hidden = hidden_f32.astype(jnp.bfloat16)
    output_rows = (
        mixed
        + lax.psum(
            jnp.dot(hidden, w_lower, preferred_element_type=jnp.float32).astype(jnp.bfloat16), "col"
        ).astype(jnp.float32)
    ).astype(jnp.bfloat16)
    grad_hidden = jnp.einsum("td,fd->tf", rows_grad, w_lower, preferred_element_type=jnp.float32)
    lower_grad = jnp.einsum("tf,td->fd", hidden, rows_grad, preferred_element_type=jnp.float32)
    grad_first, grad_second = geglu_back(grad_hidden)
    grad_both = jnp.stack([grad_first, grad_second], axis=1).astype(jnp.bfloat16)
    gate_grad = jnp.einsum("td,tgf->dgf", normed_two, grad_both, preferred_element_type=jnp.float32)
    grad_normed_two = lax.psum(
        jnp.einsum("tgf,dgf->td", grad_both, w_gate, preferred_element_type=jnp.float32), "col"
    )
    back_two, gain_mlp_part = norm_backward(grad_normed_two, gain_mlp, unit_two, inverse_two)
    grad_mixed = rows_grad.astype(jnp.float32) + back_two
    grad_mixed_low = grad_mixed.astype(jnp.bfloat16)
    proj_grad = jnp.einsum(
        "te,td->ed", attn_flat, grad_mixed_low, preferred_element_type=jnp.float32
    )
    grad_attn = jnp.einsum(
        "td,ed->te", grad_mixed_low, w_proj, preferred_element_type=jnp.float32
    ).astype(jnp.bfloat16)
    grad_by_head = lax.all_to_all(
        grad_attn.reshape(attn_rows.shape), "row", split_axis=1, concat_axis=0, tiled=True
    )
    query_grads, key_grads, value_grads = attend_back(by_head, grad_by_head, log_totals, segment)
    group_cos, group_sin = rope_tables(places, head_width)
    grad_triples = jnp.concatenate(
        [
            turn_back(query_grads, group_cos, group_sin),
            turn_back(key_grads, group_cos, group_sin),
            value_grads,
        ],
        axis=-1,
    ).astype(jnp.bfloat16)
    grad_rows_triples = lax.all_to_all(grad_triples, "row", split_axis=0, concat_axis=1, tiled=True)
    query_weight_grad = jnp.einsum(
        "td,the->dhe", normed_one, grad_rows_triples, preferred_element_type=jnp.float32
    )
    grad_normed_one = lax.psum(
        jnp.einsum(
            "the,dhe->td", grad_rows_triples, w_query, preferred_element_type=jnp.float32
        ).astype(jnp.bfloat16),
        "col",
    ).astype(jnp.float32)
    back_one, gain_attn_part = norm_backward(grad_normed_one, gain_attn, unit_one, inverse_one)
    input_rows_grad = (grad_mixed + back_one).astype(jnp.bfloat16)
    gain_attn_grad, w_qkv_grad, w_out_grad, gain_mlp_grad, w_in_grad, w_down_grad = (
        lax.psum_scatter(gain_attn_part, ("dp", "row"), scatter_dimension=0, tiled=True),
        lax.psum_scatter(query_weight_grad, ("dp", "row"), scatter_dimension=0, tiled=True),
        lax.psum_scatter(proj_grad, ("dp", "row"), scatter_dimension=1, tiled=True),
        lax.psum_scatter(gain_mlp_part, ("dp", "row"), scatter_dimension=0, tiled=True),
        lax.psum_scatter(gate_grad, ("dp", "row"), scatter_dimension=0, tiled=True),
        lax.psum_scatter(lower_grad, ("dp", "row"), scatter_dimension=1, tiled=True),
    )
    width_out, width_grad = (
        lax.all_to_all(output_rows, "row", split_axis=1, concat_axis=0, tiled=True),
        lax.all_to_all(input_rows_grad, "row", split_axis=1, concat_axis=0, tiled=True),
    )
    target = home_slots(seq_lengths, seq_offsets, deal, group_index, tokens.shape[0])
    blank_out = jnp.zeros(tokens.shape, jnp.bfloat16)
    layer_out, tokens_grad = take_rows(
        (blank_out, blank_out),
        (
            lax.all_gather(width_out, "dp", axis=0, tiled=True),
            lax.all_gather(width_grad, "dp", axis=0, tiled=True),
        ),
        target,
    )
    return (
        layer_out,
        tokens_grad,
        gain_attn_grad,
        w_qkv_grad,
        w_out_grad,
        gain_mlp_grad,
        w_in_grad,
        w_down_grad,
    )


def solution(mesh):
    return jax.shard_map(
        local,
        mesh=mesh,
        in_specs=(
            P("dp", "row"),
            P(),
            P("row", "col", None),
            P("col", "row"),
            P(),
            P("row", None, "col"),
            P("col", "row"),
            P("dp", "row"),
            P(),
            P(),
            P(),
        ),
        out_specs=(
            P("dp", "row"),
            P("dp", "row"),
            P(("dp", "row")),
            P(("dp", "row"), "col", None),
            P("col", ("dp", "row")),
            P(("dp", "row")),
            P(("dp", "row"), None, "col"),
            P("col", ("dp", "row")),
        ),
        check_vma=False,
    )
```

profile of v0, /device:TPU:0, one launch (start us, length us, event | category | flops | bytes accessed | tf_op | source)
XLA Modules:
  0.0 1970.3 jit_solution(4929160542916677543)
XLA Ops:
  12.8 176.2 %all-gather.21.cloned.1.call-done = bf16[12288,512]{1,0:T(8,128)(2,1)} async-done(((bf16[1536,512]{1,0:T(8,128)(2,1)}), bf16[12288,512]{1,0:T(8,128)(2,1)}) %all-gather.21.cloned.1.call-update) | async-done | bytes 12582928 | tf_op jit(solution)/shard_map/all_gather | solution.py:215
  200.1 165.4 %all-gather.9.cloned.1.call-done = bf16[12288,512]{1,0:T(8,128)(2,1)} async-done(((bf16[1536,512]{1,0:T(8,128)(2,1)}), bf16[12288,512]{1,0:T(8,128)(2,1)}) %all-gather.9.cloned.1.call-update) | async-done | bytes 12582928 | tf_op jit(solution)/shard_map/all_gather | solution.py:214
  383.7 35.8 %all-to-all-done = bf16[2,768,512]{2,1,0:T(8,128)(2,1)S(1)} async-done(((bf16[2,768,512]{2,1,0:T(8,128)(2,1)}), bf16[2,768,512]{2,1,0:T(8,128)(2,1)S(1)}, u32[]{:S(2)}, u32[]{:S(2)}) %all-to-all-start) | async-done | bytes 1572896 | tf_op jit(solution)/shard_map/all_to_all | solution.py:226
  448.1 32.3 %all-to-all-done.1 = bf16[768,8,192]{0,2,1:T(8,128)(2,1)S(1)} async-done(((bf16[768,8,192]{0,2,1:T(8,128)(2,1)}), bf16[768,8,192]{0,2,1:T(8,128)(2,1)S(1)}, u32[]{:S(2)}, u32[]{:S(2)}) %all-to-all-start.1) | async-done | bytes 2359328 | tf_op jit(solution)/shard_map/all_to_all | solution.py:244
  481.9 40.5 %while.27 = (s32[]{:T(128)}, bf16[3,512,4,64]{1,3,2,0:T(8,128)(2,1)S(1)}, f32[3,4,512]{2,1,0:T(4,128)S(1)}, s32[3]{0:T(128)S(1)}, s32[1536]{0:T(1024)S(1)}, /*in...) while((s32[]{:T(128)}, ...), condition=%wide.region_18.20_spmd, body=%wide.region_15.19_spmd.sunk | while | flops 843970560 | bytes 43069636 | solution.py:140
  527.0 12.0 all_to_all.139
  557.0 20.1 %all_to_all.140 = bf16[2,768,512]{2,1,0:T(8,128)(2,1)S(1)} all-to-all(bf16[2,768,512]{2,1,0:T(8,128)(2,1)} %bitcast.261), channel_id=1, replica_groups=mesh['dp'=8,'row'=2,'col'=2] {'row'}, dimensions={0} | all-to-all | bytes 3145728 | tf_op jit(solution)/shard_map/all_to_all | solution.py:227
  593.4 55.1 %all-gather.15.cloned.1.call-done = bf16[1024,2,1312]{0,2,1:T(8,128)(2,1)} async-done(((bf16[512,2,1312]{0,2,1:T(8,128)(2,1)}), bf16[1024,2,1312]{0,2,1:T(8,128)(2,1)}) %all-gather.15.cloned.1.call-update) | async-done | bytes 5373968 | tf_op jit(solution)/shard_map/all_gather | solution.py:222
  678.5 23.4 %all-reduce.10.cloned.1.call-done = f32[768,1024]{1,0:T(8,128)} async-done(((f32[768,1024]{1,0:T(8,128)}), f32[768,1024]{1,0:T(8,128)}) %all-reduce.10.cloned.1.call-update) | async-done | bytes 3145744 | tf_op jit(solution)/shard_map/psum | solution.py:265
  733.2 110.9 %while.28 = (s32[]{:T(128)}, f32[1536,4,64]{0,2,1:T(8,128)}, f32[1536,4,64]{0,2,1:T(8,128)}, f32[3,512,4,64]{1,0,3,2:T(4,128)}, s32[3]{0:T(128)S(1)}, /*index=5*...) while((s32[]{:T(128)}, f32[1536,4,64]{0,2,1:T(8,128)}, ...), condition=%wide.region_28.30_spmd.clone, body=%wide.region_26.29_spmd.clone.sunk | while | flops 2044459008 | bytes 139776368 | solution.py:187
  758.4 11.1 dynamic_update_slice.20
  833.1 11.1 dynamic_update_slice.20
  873.6 26.5 %all-to-all-done.6 = bf16[1536,4,192]{2,1,0:T(4,128)(2,1)S(1)} async-done(((bf16[1536,4,192]{2,1,0:T(4,128)(2,1)}), bf16[1536,4,192]{2,1,0:T(4,128)(2,1)S(1)}, u32[]{:S(2)}, u32[]{:S(2)}) %all-to-all-start.6) | async-done | bytes 2359328 | tf_op jit(solution)/shard_map/all_to_all | solution.py:290
  920.6 13.0 fusion.71
  937.1 56.3 %all_to_all.141 = bf16[768,2,512]{2,0,1:T(8,128)(2,1)} all-to-all(bf16[768,2,512]{2,0,1:T(8,128)(2,1)S(1)} %bitcast.259), channel_id=1, replica_groups=mesh['dp'=8,'row'=2,'col'=2] {'row'}, dimensions={1} | all-to-all | bytes 3145728 | tf_op jit(solution)/shard_map/all_to_all | solution.py:311
  997.8 55.0 %all_to_all.142 = bf16[768,2,512]{2,0,1:T(8,128)(2,1)} all-to-all(bf16[768,2,512]{2,0,1:T(8,128)(2,1)S(1)} %bitcast.260), channel_id=1, replica_groups=mesh['dp'=8,'row'=2,'col'=2] {'row'}, dimensions={1} | all-to-all | bytes 3145728 | tf_op jit(solution)/shard_map/all_to_all | solution.py:312
  1056.5 16.5 fusion.76
  1075.7 46.4 %all-reduce.2 = (f32[1024]{0:T(1024)S(1)}, f32[1024]{0:T(1024)S(1)}) all-reduce(f32[1024]{0:T(1024)S(1)} %get-tuple-element.202, f32[1024]{0:T(1024)S(1)} %copy-done.39), channel_id=2, replica_groups=mesh['dp'=8,'row'=2,'col'=2] {'dp','row'}, use_global_device_ids=true, to_apply=%region_33.35.clone | all-reduce | flops 2048 | bytes 16384
  1123.3 26.9 %reduce-scatter.5.cloned.1.call-done = f32[64,8,192]{2,0,1:T(8,128)} async-done(((f32[1024,8,192]{2,0,1:T(8,128)}), f32[64,8,192]{2,0,1:T(8,128)}) %reduce-scatter.5.cloned.1.call-update) | async-done | bytes 393232 | tf_op jit(solution)/shard_map/reduce_scatter | solution.py:304
  1152.4 244.7 %reduce-scatter.9.cloned.1.call-done = f32[64,2,1312]{2,0,1:T(8,128)} async-done(((f32[1024,2,1312]{2,0,1:T(8,128)}), f32[64,2,1312]{2,0,1:T(8,128)}) %reduce-scatter.9.cloned.1.call-update) | async-done | bytes 671760 | tf_op jit(solution)/shard_map/reduce_scatter | solution.py:307
  1399.6 179.3 %all-gather.19.cloned.1.call-done = bf16[12288,512]{1,0:T(8,128)(2,1)} async-done(((bf16[1536,512]{1,0:T(8,128)(2,1)}), bf16[12288,512]{1,0:T(8,128)(2,1)}) %all-gather.19.cloned.1.call-update) | async-done | bytes 12582928 | tf_op jit(solution)/shard_map/all_gather | solution.py:319
  1590.0 165.4 %all-gather.23.cloned.1.call-done = bf16[12288,512]{1,0:T(8,128)(2,1)} async-done(((bf16[1536,512]{1,0:T(8,128)(2,1)}), bf16[12288,512]{1,0:T(8,128)(2,1)}) %all-gather.23.cloned.1.call-update) | async-done | bytes 12582928 | tf_op jit(solution)/shard_map/all_gather | solution.py:320
  1768.9 68.9 %reduce-scatter.7.cloned.1.call-done = f32[512,64]{0,1:T(8,128)} async-done(((f32[512,1024]{0,1:T(8,128)}), f32[512,64]{0,1:T(8,128)}) %reduce-scatter.7.cloned.1.call-update) | async-done | bytes 131088 | tf_op jit(solution)/shard_map/reduce_scatter | solution.py:305
  1837.8 125.6 %reduce-scatter.11.cloned.1.call-done = f32[1312,64]{0,1:T(8,128)} async-done(((f32[1312,1024]{0,1:T(8,128)}), f32[1312,64]{0,1:T(8,128)}) %reduce-scatter.11.cloned.1.call-update) | async-done | bytes 335888 | tf_op jit(solution)/shard_map/reduce_scatter | solution.py:308
  (311 shorter events, 377.4 us)
Async XLA Ops:
  7.2 181.9 %all-gather.21.cloned.1.call-start = ((), (), s32[]{:S(2)}) async-start(), calls=%async_computation.19 | async-start | bytes 14155776 | tf_op jit(solution)/shard_map/all_gather | solution.py:215
  7.9 357.6 %all-gather.9.cloned.1.call-start = ((), (), s32[]{:S(2)}) async-start(), calls=%async_computation.12 | async-start | bytes 14155776 | tf_op jit(solution)/shard_map/all_gather | solution.py:214
  8.7 420.8 %all-gather.11.cloned.1.call-start = ((), (), s32[]{:S(2)}) async-start(), calls=%async_computation.13 | async-start | bytes 4718592 | tf_op jit(solution)/shard_map/all_gather | solution.py:220
  378.9 40.6 %all-to-all-start = ((bf16[2,768,512]{2,1,0:T(8,128)(2,1)}), bf16[2,768,512]{2,1,0:T(8,128)(2,1)S(1)}, u32[]{:S(2)}, u32[]{:S(2)}) async-start(bf16[2,768,512]{2,1,0:T(8,128)(2,1)} %bitcast.262), calls=%async_computation | async-start | bytes 3145728 | tf_op jit(solution)/shard_map/all_to_all | solution.py:226
  438.8 41.6 %all-to-all-start.1 = ((bf16[768,8,192]{0,2,1:T(8,128)(2,1)}), bf16[768,8,192]{0,2,1:T(8,128)(2,1)S(1)}, u32[]{:S(2)}, u32[]{:S(2)}) async-start(bf16[768,8,192]{0,2,1:T(8,128)(2,1)} %fusion.89), calls=%async_computation.1 | async-start | bytes 4718592 | tf_op jit(solution)/shard_map/all_to_all | solution.py:244
  442.6 105.7 %all-gather.13.cloned.1.call-start = ((), (), s32[]{:S(2)}) async-start(), calls=%async_computation.14 | async-start | bytes 1572864 | tf_op jit(solution)/shard_map/all_gather | solution.py:221
  444.9 133.5 %all-gather.17.cloned.1.call-start = ((), (), s32[]{:S(2)}) async-start(), calls=%async_computation.17 | async-start | bytes 4030464 | tf_op jit(solution)/shard_map/all_gather | solution.py:223
  448.0 136.9 %all-reduce.8.cloned.1.call-start = ((), (), s32[]{:S(2)}) async-start(), calls=%async_computation.15 | async-start | bytes 6291456 | tf_op jit(solution)/shard_map/psum | solution.py:248
  552.5 96.1 %all-gather.15.cloned.1.call-start = ((), (), s32[]{:S(2)}) async-start(), calls=%async_computation.16 | async-start | bytes 8060928 | tf_op jit(solution)/shard_map/all_gather | solution.py:222
  557.0 144.9 %all-reduce.10.cloned.1.call-start = ((), (), s32[]{:S(2)}) async-start(), calls=%async_computation.20 | async-start | bytes 6291456 | tf_op jit(solution)/shard_map/psum | solution.py:265
  590.8 57.8 %copy-start.37 = (f32[1024]{0:T(1024)S(1)}, f32[1024]{0:T(1024)}, u32[]{:S(2)}) copy-start(f32[1024]{0:T(1024)} %param.21) | copy-start | bytes 12292
  590.8 115.9 %copy-start.28 = (f32[768]{0:T(1024)}, f32[768]{0:T(1024)S(1)}, u32[]{:S(2)}) copy-start(f32[768]{0:T(1024)S(1)} %broadcast_multiply_fusion.4) | copy-start | bytes 9220
  593.4 113.2 %copy-start.32 = (f32[768]{0:T(1024)}, f32[768]{0:T(1024)S(1)}, u32[]{:S(2)}) copy-start(f32[768]{0:T(1024)S(1)} %add_rsqrt_fusion) | copy-start | bytes 9220
  713.0 15.0 all-to-all-start.5
  860.2 39.9 %all-to-all-start.6 = ((bf16[1536,4,192]{2,1,0:T(4,128)(2,1)}), bf16[1536,4,192]{2,1,0:T(4,128)(2,1)S(1)}, u32[]{:S(2)}, u32[]{:S(2)}) async-start(bf16[1536,4,192]{2,1,0:T(4,128)(2,1)} %copy.115), calls=%async_computation.6 | async-start | bytes 6291456 | tf_op jit(solution)/shard_map/all_to_all | solution.py:290
  864.1 69.9 %all-reduce.12.cloned.1.call-start = ((), (), s32[]{:S(2)}) async-start(), calls=%async_computation.26 | async-start | bytes 6291456 | tf_op jit(solution)/shard_map/psum | solution.py:256
  910.2 240.0 %reduce-scatter.5.cloned.1.call-start = ((), (), s32[]{:S(2)}) async-start(), calls=%async_computation.22 | async-start | bytes 8912896 | tf_op jit(solution)/shard_map/reduce_scatter | solution.py:304
  918.9 478.2 %reduce-scatter.9.cloned.1.call-start = ((), (), s32[]{:S(2)}) async-start(), calls=%async_computation.24 | async-start | bytes 12255232 | tf_op jit(solution)/shard_map/reduce_scatter | solution.py:307
  933.6 645.3 %all-gather.19.cloned.1.call-start = ((), (), s32[]{:S(2)}) async-start(), calls=%async_computation.18 | async-start | bytes 14155776 | tf_op jit(solution)/shard_map/all_gather | solution.py:319
  937.1 56.4 %copy-start.5 = (f32[768,1024]{1,0:T(8,128)S(1)}, f32[768,1024]{1,0:T(8,128)}, u32[]{:S(2)}) copy-start(f32[768,1024]{1,0:T(8,128)} %copy-done.4) | copy-start | bytes 9437188
  993.4 762.1 %all-gather.23.cloned.1.call-start = ((), (), s32[]{:S(2)}) async-start(), calls=%async_computation.21 | async-start | bytes 14155776 | tf_op jit(solution)/shard_map/all_gather | solution.py:320
  997.8 55.1 %copy-start.10 = (f32[768,1024]{1,0:T(8,128)S(1)}, f32[768,1024]{1,0:T(8,128)}, u32[]{:S(2)}) copy-start(f32[768,1024]{1,0:T(8,128)} %copy-done.8) | copy-start | bytes 9437188
  1052.8 784.9 %reduce-scatter.7.cloned.1.call-start = ((), (), s32[]{:S(2)}) async-start(), calls=%async_computation.23 | async-start | bytes 2228224 | tf_op jit(solution)/shard_map/reduce_scatter | solution.py:305
  1056.4 906.9 %reduce-scatter.11.cloned.1.call-start = ((), (), s32[]{:S(2)}) async-start(), calls=%async_computation.25 | async-start | bytes 6127616 | tf_op jit(solution)/shard_map/reduce_scatter | solution.py:308
  (50 other events, 202.2 us)
Sparse Core Ops, SparseCore 0:
  10.2 178.8 all-gather.20
  191.2 174.2 all-gather.8
  367.1 59.9 all-gather.10
  445.2 31.5 all-gather.12
  478.2 39.7 all-gather.16
  552.6 23.1 all-reduce.7
  577.3 71.1 all-gather.14
  678.6 23.2 all-reduce.9
  910.3 23.6 all-reduce.11
  936.2 214.0 reduce-scatter.4
  1152.5 244.5 reduce-scatter.8
  1399.2 179.7 all-gather.18
  1581.2 174.2 all-gather.22
  1758.2 79.5 reduce-scatter.6
  1840.5 122.7 reduce-scatter.10
where the time goes:
time: 1980 us; the launch traced here: 1970 us
  waiting for transfers between devices  1340 us (68%)
  blocking collectives  190 us (10%)
  matrix products  166 us (8%)
  local copies, waits for them, and re-layouts  138 us (7%)
  other arithmetic  97.8 us (5%)
    reduce_scatter x1, waiting for transfers between devices, local(): lax.psum_scatter(gate_grad, ('dp', 'row'), scatter_dimension=0, tiled=True)  245 us
    all_gather x1, waiting for transfers between devices, local(): lax.all_gather(width_out, 'dp', axis=0, tiled=True)  179 us
    all_gather x1, waiting for transfers between devices, local(): lax.all_gather(cotangent, 'dp', axis=0, tiled=True)  176 us
    all_gather x1, waiting for transfers between devices, local(): lax.all_gather(width_grad, 'dp', axis=0, tiled=True)  165 us
    all_gather x1, waiting for transfers between devices, local(): lax.all_gather(tokens, 'dp', axis=0, tiled=True)  165 us
    reduce_scatter x1, waiting for transfers between devices, local(): lax.psum_scatter(lower_grad, ('dp', 'row'), scatter_dimension=1, tiled=True)  126 us
    reduce_scatter x1, waiting for transfers between devices, local(): lax.psum_scatter(proj_grad, ('dp', 'row'), scatter_dimension=1, tiled=True)  68.9 us
    all_to_all x1, blocking collectives, local(): lax.all_to_all(output_rows, 'row', split_axis=1, concat_axis=0, tiled=True)  56.3 us
  transfers between devices with their start and end apart: 19, of which 15 were waited for; matrix products, arithmetic and copies ran while one was open for 11% of the time, Pallas kernels for 0%

commit v1 on v0

--- a/solution.py
+++ b/solution.py
@@ -313,12 +313,28 @@
     )
     target = home_slots(seq_lengths, seq_offsets, deal, group_index, tokens.shape[0])
     blank_out = jnp.zeros(tokens.shape, jnp.bfloat16)
+
+    def post_state_on(slab_in):
+        n_shards = lax.axis_size("dp")
+        seen = tuple(((ix, (ix + 1) % n_shards) for ix in range(n_shards)))
+        store = tuple(((ix, (ix - 1) % n_shards) for ix in range(n_shards)))
+        left_arr, local_out = ([slab_in], [slab_in])
+        for _ in range(n_shards // 2):
+            long_array = lax.ppermute(left_arr[-1], axis_name="dp", perm=seen)
+            left_arr.append(long_array)
+        i0 = 0
+        while i0 < (n_shards - 1) // 2:
+            s_next = lax.ppermute(local_out[-1], axis_name="dp", perm=store)
+            local_out.append(s_next)
+            i0 += 1
+        q_next = jnp.concatenate([*left_arr[::-1], *local_out[1:]], 0)
+        wide_out = lax.axis_index("dp")
+        top = jnp.roll(q_next, (wide_out - n_shards // 2) * slab_in.shape[0], 0)
+        return top
+
     layer_out, tokens_grad = take_rows(
         (blank_out, blank_out),
-        (
-            lax.all_gather(width_out, "dp", axis=0, tiled=True),
-            lax.all_gather(width_grad, "dp", axis=0, tiled=True),
-        ),
+        (post_state_on(width_out), lax.all_gather(width_grad, "dp", axis=0, tiled=True)),
         target,
     )
     return (

time: 1980 us -> 1840 us (0.929)
  waiting for transfers between devices: 1340 us -> 1060 us
  blocking collectives: 190 us -> 283 us
  starting transfers between devices: 16.1 us -> 39.4 us
  local copies, waits for them, and re-layouts: 138 us -> 158 us
    ppermute x0 -> x7, waiting for transfers between devices: none -> 256 us  [the longest x4 158 us: post_state_on(): long_array = lax.ppermute(left_arr[-1], axis_name='dp', perm=seen)]
    reduce_scatter x1, waiting for transfers between devices: 245 us -> 0.01 us  [local(): lax.psum_scatter(gate_grad, ('dp', 'row'), scatter_dimension=0, tiled=True)]
    all_gather x1 -> x0, waiting for transfers between devices: 179 us -> none  [local(): lax.all_gather(width_out, 'dp', axis=0, tiled=True)]
    unnamed x1, blocking collectives: 46.4 us -> 137 us
    all_gather x1, waiting for transfers between devices: 165 us -> 82.4 us  [local(): lax.all_gather(width_grad, 'dp', axis=0, tiled=True)]
    reduce_scatter x1, waiting for transfers between devices: 26.9 us -> 0.02 us  [local(): lax.psum_scatter(query_weight_grad, ('dp', 'row'), scatter_dimension=0, t...]
    ppermute x0 -> x7, starting transfers between devices: none -> 23.3 us  [the longest x3 14.8 us: post_state_on(): s_next = lax.ppermute(local_out[-1], axis_name='dp', perm=store)]
  transfers between devices with their start and end apart: 19 -> 25, of which waited for: 15 -> 16; matrix products, arithmetic and copies ran while one was open for 11% -> 13% of each run, Pallas kernels for 0% -> 0%
where the time goes in v1:
time: 1840 us; the launch traced here: 1830 us
  waiting for transfers between devices  1060 us (58%)
  blocking collectives  283 us (15%)
  matrix products  167 us (9%)
  local copies, waits for them, and re-layouts  158 us (9%)
  other arithmetic  98.1 us (5%)
  starting transfers between devices  39.4 us (2%)
    all_gather x1, waiting for transfers between devices, local(): lax.all_gather(cotangent, 'dp', axis=0, tiled=True)  176 us
    all_gather x1, waiting for transfers between devices, local(): lax.all_gather(tokens, 'dp', axis=0, tiled=True)  165 us
    ppermute x4, waiting for transfers between devices, post_state_on(): long_array = lax.ppermute(left_arr[-1], axis_name='dp', perm=seen)  158 us
    unnamed x1, blocking collectives  137 us
    reduce_scatter x1, waiting for transfers between devices, local(): lax.psum_scatter(lower_grad, ('dp', 'row'), scatter_dimension=1, tiled=True)  125 us
    ppermute x3, waiting for transfers between devices, post_state_on(): s_next = lax.ppermute(local_out[-1], axis_name='dp', perm=store)  98.2 us
    all_gather x1, waiting for transfers between devices, local(): lax.all_gather(width_grad, 'dp', axis=0, tiled=True)  82.4 us
    reduce_scatter x1, waiting for transfers between devices, local(): lax.psum_scatter(proj_grad, ('dp', 'row'), scatter_dimension=1, tiled=True)  69.1 us
  transfers between devices with their start and end apart: 25, of which 16 were waited for; matrix products, arithmetic and copies ran while one was open for 13% of the time, Pallas kernels for 0%

profile of v1, /device:TPU:0, one launch (start us, length us, event | category | flops | bytes accessed | tf_op | source)
XLA Modules:
  0.0 1830.7 jit_solution(3743099029709377085)
XLA Ops:
  12.8 176.2 %all-gather.18.cloned.1.call-done = bf16[12288,512]{1,0:T(8,128)(2,1)} async-done(((bf16[1536,512]{1,0:T(8,128)(2,1)}), bf16[12288,512]{1,0:T(8,128)(2,1)}) %all-gather.18.cloned.1.call-update) | async-done | bytes 12582928 | tf_op jit(solution)/shard_map/all_gather | solution.py:215
  200.1 165.4 %all-gather.8.cloned.1.call-done = bf16[12288,512]{1,0:T(8,128)(2,1)} async-done(((bf16[1536,512]{1,0:T(8,128)(2,1)}), bf16[12288,512]{1,0:T(8,128)(2,1)}) %all-gather.8.cloned.1.call-update) | async-done | bytes 12582928 | tf_op jit(solution)/shard_map/all_gather | solution.py:214
  383.7 35.8 %all-to-all-done = bf16[2,768,512]{2,1,0:T(8,128)(2,1)S(1)} async-done(((bf16[2,768,512]{2,1,0:T(8,128)(2,1)}), bf16[2,768,512]{2,1,0:T(8,128)(2,1)S(1)}, u32[]{:S(2)}, u32[]{:S(2)}) %all-to-all-start) | async-done | bytes 1572896 | tf_op jit(solution)/shard_map/all_to_all | solution.py:226
  448.2 32.2 %all-to-all-done.1 = bf16[768,8,192]{0,2,1:T(8,128)(2,1)S(1)} async-done(((bf16[768,8,192]{0,2,1:T(8,128)(2,1)}), bf16[768,8,192]{0,2,1:T(8,128)(2,1)S(1)}, u32[]{:S(2)}, u32[]{:S(2)}) %all-to-all-start.1) | async-done | bytes 2359328 | tf_op jit(solution)/shard_map/all_to_all | solution.py:244
  482.0 40.5 %while.27 = (s32[]{:T(128)}, bf16[3,512,4,64]{1,3,2,0:T(8,128)(2,1)S(1)}, f32[3,4,512]{2,1,0:T(4,128)S(1)}, s32[3]{0:T(128)S(1)}, s32[1536]{0:T(1024)S(1)}, /*in...) while((s32[]{:T(128)}, ...), condition=%wide.region_18.20_spmd, body=%wide.region_15.19_spmd.sunk | while | flops 843970560 | bytes 43069636 | solution.py:140
  527.1 12.0 all_to_all.139
  557.2 20.1 %all_to_all.140 = bf16[2,768,512]{2,1,0:T(8,128)(2,1)S(1)} all-to-all(bf16[2,768,512]{2,1,0:T(8,128)(2,1)} %bitcast.264), channel_id=1, replica_groups=mesh['dp'=8,'row'=2,'col'=2] {'row'}, dimensions={0} | all-to-all | bytes 3145728 | tf_op jit(solution)/shard_map/all_to_all | solution.py:227
  593.6 55.1 %all-gather.14.cloned.1.call-done = bf16[1024,2,1312]{0,2,1:T(8,128)(2,1)} async-done(((bf16[512,2,1312]{0,2,1:T(8,128)(2,1)}), bf16[1024,2,1312]{0,2,1:T(8,128)(2,1)}) %all-gather.14.cloned.1.call-update) | async-done | bytes 5373968 | tf_op jit(solution)/shard_map/all_gather | solution.py:222
  678.8 23.4 %all-reduce.10.cloned.1.call-done = f32[768,1024]{1,0:T(8,128)} async-done(((f32[768,1024]{1,0:T(8,128)}), f32[768,1024]{1,0:T(8,128)}) %all-reduce.10.cloned.1.call-update) | async-done | bytes 3145744 | tf_op jit(solution)/shard_map/psum | solution.py:265
  733.9 111.1 %while.28 = (s32[]{:T(128)}, f32[1536,4,64]{0,2,1:T(8,128)}, f32[1536,4,64]{0,2,1:T(8,128)}, f32[3,512,4,64]{1,0,3,2:T(4,128)}, s32[3]{0:T(128)S(1)}, /*index=5*...) while((s32[]{:T(128)}, f32[1536,4,64]{0,2,1:T(8,128)}, ...), condition=%wide.region_28.30_spmd.clone, body=%wide.region_26.29_spmd.clone.sunk | while | flops 2044459008 | bytes 139776368 | solution.py:187
  874.3 26.5 %all-to-all-done.6 = bf16[1536,4,192]{2,1,0:T(4,128)(2,1)S(1)} async-done(((bf16[1536,4,192]{2,1,0:T(4,128)(2,1)}), bf16[1536,4,192]{2,1,0:T(4,128)(2,1)S(1)}, u32[]{:S(2)}, u32[]{:S(2)}) %all-to-all-start.6) | async-done | bytes 2359328 | tf_op jit(solution)/shard_map/all_to_all | solution.py:290
  920.5 13.3 fusion.71
  940.2 58.4 %all_to_all.141 = bf16[768,2,512]{2,0,1:T(8,128)(2,1)} all-to-all(bf16[768,2,512]{2,0,1:T(8,128)(2,1)S(1)} %bitcast.262), channel_id=1, replica_groups=mesh['dp'=8,'row'=2,'col'=2] {'row'}, dimensions={1} | all-to-all | bytes 3145728 | tf_op jit(solution)/shard_map/all_to_all | solution.py:312
  1001.3 55.2 %all_to_all.142 = bf16[768,2,512]{2,0,1:T(8,128)(2,1)S(1)} all-to-all(bf16[768,2,512]{2,0,1:T(8,128)(2,1)S(1)} %bitcast.263), channel_id=1, replica_groups=mesh['dp'=8,'row'=2,'col'=2] {'row'}, dimensions={1} | all-to-all | bytes 3145728 | tf_op jit(solution)/shard_map/all_to_all | solution.py:311
  1064.4 62.4 %collective-permute-done = bf16[1536,512]{1,0:T(8,128)(2,1)} collective-permute-done((bf16[1536,512]{1,0:T(8,128)(2,1)S(1)}, bf16[1536,512]{1,0:T(8,128)(2,1)}, u32[]{:S(2)}, u32[]{:S(2)}) %collective-permute-start) | collective-permute-done | bytes 1572896 | tf_op jit(solution)/shard_map/ppermute | solution.py:323
  1127.3 16.1 fusion.76
  1149.0 95.8 %collective-permute-done.1 = bf16[1536,512]{1,0:T(8,128)(2,1)} collective-permute-done((bf16[1536,512]{1,0:T(8,128)(2,1)}, bf16[1536,512]{1,0:T(8,128)(2,1)}, u32[]{:S(2)}, u32[]{:S(2)}) %collective-permute-start.1) | collective-permute-done | bytes 1572896 | tf_op jit(solution)/shard_map/ppermute | solution.py:323
  1247.4 70.4 %collective-permute-done.4 = bf16[1536,512]{1,0:T(8,128)(2,1)S(1)} collective-permute-done((bf16[1536,512]{1,0:T(8,128)(2,1)S(1)}, bf16[1536,512]{1,0:T(8,128)(2,1)S(1)}, u32[]{:S(2)}, u32[]{:S(2)}) %collective-permute-start.4) | collective-permute-done | bytes 1572896 | tf_op jit(solution)/shard_map/ppermute | solution.py:327
  1322.2 137.3 %all-reduce.2 = (f32[1024]{0:T(1024)S(1)}, f32[1024]{0:T(1024)S(1)}) all-reduce(f32[1024]{0:T(1024)S(1)} %get-tuple-element.202, f32[1024]{0:T(1024)S(1)} %copy-done.40), channel_id=2, replica_groups=mesh['dp'=8,'row'=2,'col'=2] {'dp','row'}, use_global_device_ids=true, to_apply=%region_33.35.clone | all-reduce | flops 2048 | bytes 16384
  1475.5 27.8 %collective-permute-done.6 = bf16[1536,512]{1,0:T(8,128)(2,1)S(1)} collective-permute-done((bf16[1536,512]{1,0:T(8,128)(2,1)}, bf16[1536,512]{1,0:T(8,128)(2,1)S(1)}, u32[]{:S(2)}, u32[]{:S(2)}) %collective-permute-start.6) | collective-permute-done | bytes 1572896 | tf_op jit(solution)/shard_map/ppermute | solution.py:327
  1518.3 11.1 gather_fusion.1
  1534.1 82.4 %all-gather.20.cloned.1.call-done = bf16[12288,512]{1,0:T(8,128)(2,1)} async-done(((bf16[1536,512]{1,0:T(8,128)(2,1)}), bf16[12288,512]{1,0:T(8,128)(2,1)}) %all-gather.20.cloned.1.call-update) | async-done | bytes 12582928 | tf_op jit(solution)/shard_map/all_gather | solution.py:337
  1629.9 69.1 %reduce-scatter.7.cloned.1.call-done = f32[512,64]{0,1:T(8,128)} async-done(((f32[512,1024]{0,1:T(8,128)}), f32[512,64]{0,1:T(8,128)}) %reduce-scatter.7.cloned.1.call-update) | async-done | bytes 131088 | tf_op jit(solution)/shard_map/reduce_scatter | solution.py:305
  1698.9 124.8 %reduce-scatter.11.cloned.1.call-done = f32[1312,64]{0,1:T(8,128)} async-done(((f32[1312,1024]{0,1:T(8,128)}), f32[1312,64]{0,1:T(8,128)}) %reduce-scatter.11.cloned.1.call-update) | async-done | bytes 335888 | tf_op jit(solution)/shard_map/reduce_scatter | solution.py:308
  (341 shorter events, 433.9 us)
Async XLA Ops:
  7.2 181.9 %all-gather.18.cloned.1.call-start = ((), (), s32[]{:S(2)}) async-start(), calls=%async_computation.18 | async-start | bytes 14155776 | tf_op jit(solution)/shard_map/all_gather | solution.py:215
  7.9 357.6 %all-gather.8.cloned.1.call-start = ((), (), s32[]{:S(2)}) async-start(), calls=%async_computation.12 | async-start | bytes 14155776 | tf_op jit(solution)/shard_map/all_gather | solution.py:214
  8.7 420.8 %all-gather.10.cloned.1.call-start = ((), (), s32[]{:S(2)}) async-start(), calls=%async_computation.13 | async-start | bytes 4718592 | tf_op jit(solution)/shard_map/all_gather | solution.py:220
  378.9 40.6 %all-to-all-start = ((bf16[2,768,512]{2,1,0:T(8,128)(2,1)}), bf16[2,768,512]{2,1,0:T(8,128)(2,1)S(1)}, u32[]{:S(2)}, u32[]{:S(2)}) async-start(bf16[2,768,512]{2,1,0:T(8,128)(2,1)} %bitcast.265), calls=%async_computation | async-start | bytes 3145728 | tf_op jit(solution)/shard_map/all_to_all | solution.py:226
  438.8 41.6 %all-to-all-start.1 = ((bf16[768,8,192]{0,2,1:T(8,128)(2,1)}), bf16[768,8,192]{0,2,1:T(8,128)(2,1)S(1)}, u32[]{:S(2)}, u32[]{:S(2)}) async-start(bf16[768,8,192]{0,2,1:T(8,128)(2,1)} %fusion.89), calls=%async_computation.1 | async-start | bytes 4718592 | tf_op jit(solution)/shard_map/all_to_all | solution.py:244
  442.6 105.8 %all-gather.12.cloned.1.call-start = ((), (), s32[]{:S(2)}) async-start(), calls=%async_computation.14 | async-start | bytes 1572864 | tf_op jit(solution)/shard_map/all_gather | solution.py:221
  445.0 133.6 %all-gather.16.cloned.1.call-start = ((), (), s32[]{:S(2)}) async-start(), calls=%async_computation.17 | async-start | bytes 4030464 | tf_op jit(solution)/shard_map/all_gather | solution.py:223
  448.1 137.0 %all-reduce.8.cloned.1.call-start = ((), (), s32[]{:S(2)}) async-start(), calls=%async_computation.15 | async-start | bytes 6291456 | tf_op jit(solution)/shard_map/psum | solution.py:248
  552.6 96.1 %all-gather.14.cloned.1.call-start = ((), (), s32[]{:S(2)}) async-start(), calls=%async_computation.16 | async-start | bytes 8060928 | tf_op jit(solution)/shard_map/all_gather | solution.py:222
  557.2 145.1 %all-reduce.10.cloned.1.call-start = ((), (), s32[]{:S(2)}) async-start(), calls=%async_computation.19 | async-start | bytes 6291456 | tf_op jit(solution)/shard_map/psum | solution.py:265
  860.9 39.9 %all-to-all-start.6 = ((bf16[1536,4,192]{2,1,0:T(4,128)(2,1)}), bf16[1536,4,192]{2,1,0:T(4,128)(2,1)S(1)}, u32[]{:S(2)}, u32[]{:S(2)}) async-start(bf16[1536,4,192]{2,1,0:T(4,128)(2,1)} %copy.115), calls=%async_computation.6 | async-start | bytes 6291456 | tf_op jit(solution)/shard_map/all_to_all | solution.py:290
  864.9 70.0 %all-reduce.12.cloned.1.call-start = ((), (), s32[]{:S(2)}) async-start(), calls=%async_computation.25 | async-start | bytes 6291456 | tf_op jit(solution)/shard_map/psum | solution.py:256
  911.1 618.3 %reduce-scatter.5.cloned.1.call-start = ((), (), s32[]{:S(2)}) async-start(), calls=%async_computation.21 | async-start | bytes 8912896 | tf_op jit(solution)/shard_map/reduce_scatter | solution.py:304
  919.0 612.6 %reduce-scatter.9.cloned.1.call-start = ((), (), s32[]{:S(2)}) async-start(), calls=%async_computation.23 | async-start | bytes 12255232 | tf_op jit(solution)/shard_map/reduce_scatter | solution.py:307
  933.9 682.6 %all-gather.20.cloned.1.call-start = ((), (), s32[]{:S(2)}) async-start(), calls=%async_computation.20 | async-start | bytes 14155776 | tf_op jit(solution)/shard_map/all_gather | solution.py:337
  998.6 700.3 %reduce-scatter.7.cloned.1.call-start = ((), (), s32[]{:S(2)}) async-start(), calls=%async_computation.22 | async-start | bytes 2228224 | tf_op jit(solution)/shard_map/reduce_scatter | solution.py:305
  1056.5 70.3 %collective-permute-start = (bf16[1536,512]{1,0:T(8,128)(2,1)S(1)}, bf16[1536,512]{1,0:T(8,128)(2,1)}, u32[]{:S(2)}, u32[]{:S(2)}) collective-permute-start(bf16[1536,512]{1,0:T(8,128)(2,1)S(1)} %bitcast.241), channel_id=1, source_target_pairs={{0,4},{4,8},{8,12},{12,16},{16,20},{20,24},{24,28},{28,0},{1,5},{5... | collective-permute-start | bytes 4718600 | tf_op jit(solution)/shard_map/ppermute | solution.py:323
  1064.3 759.4 %reduce-scatter.11.cloned.1.call-start = ((), (), s32[]{:S(2)}) async-start(), calls=%async_computation.24 | async-start | bytes 6127616 | tf_op jit(solution)/shard_map/reduce_scatter | solution.py:308
  1126.8 118.0 %collective-permute-start.1 = (bf16[1536,512]{1,0:T(8,128)(2,1)}, bf16[1536,512]{1,0:T(8,128)(2,1)}, u32[]{:S(2)}, u32[]{:S(2)}) collective-permute-start(bf16[1536,512]{1,0:T(8,128)(2,1)} %collective-permute-done), channel_id=1, source_target_pairs={{0,4},{4,8},{8,12},{12,16},{16,20},{20,24},{24,28},{28,0},{1,5},{5... | collective-permute-start | bytes 4718600 | tf_op jit(solution)/shard_map/ppermute | solution.py:323
  1143.4 174.4 %collective-permute-start.4 = (bf16[1536,512]{1,0:T(8,128)(2,1)S(1)}, bf16[1536,512]{1,0:T(8,128)(2,1)S(1)}, u32[]{:S(2)}, u32[]{:S(2)}) collective-permute-start(bf16[1536,512]{1,0:T(8,128)(2,1)S(1)} %bitcast.242), channel_id=1, source_target_pairs={{0,28},{4,0},{8,4},{12,8},{16,12},{20,16},{24,20},{28,24},{1,29},{... | collective-permute-start | bytes 4718600 | tf_op jit(solution)/shard_map/ppermute | solution.py:327
  1244.8 75.3 %collective-permute-start.2 = (bf16[1536,512]{1,0:T(8,128)(2,1)}, bf16[1536,512]{1,0:T(8,128)(2,1)}, u32[]{:S(2)}, u32[]{:S(2)}) collective-permute-start(bf16[1536,512]{1,0:T(8,128)(2,1)} %collective-permute-done.1), channel_id=1, source_target_pairs={{0,4},{4,8},{8,12},{12,16},{16,20},{20,24},{24,28},{28,0},{1,5},{5... | collective-permute-start | bytes 4718600 | tf_op jit(solution)/shard_map/ppermute | solution.py:323
  1317.9 142.8 %collective-permute-start.5 = (bf16[1536,512]{1,0:T(8,128)(2,1)S(1)}, bf16[1536,512]{1,0:T(8,128)(2,1)}, u32[]{:S(2)}, u32[]{:S(2)}) collective-permute-start(bf16[1536,512]{1,0:T(8,128)(2,1)S(1)} %collective-permute-done.4), channel_id=1, source_target_pairs={{0,28},{4,0},{8,4},{12,8},{16,12},{20,16},{24,20},{28,24},{1,29},{... | collective-permute-start | bytes 4718600 | tf_op jit(solution)/shard_map/ppermute | solution.py:327
  1320.0 147.6 %collective-permute-start.3 = (bf16[1536,512]{1,0:T(8,128)(2,1)}, bf16[1536,512]{1,0:T(8,128)(2,1)}, u32[]{:S(2)}, u32[]{:S(2)}) collective-permute-start(bf16[1536,512]{1,0:T(8,128)(2,1)} %collective-permute-done.2), channel_id=1, source_target_pairs={{0,4},{4,8},{8,12},{12,16},{16,20},{20,24},{24,28},{28,0},{1,5},{5... | collective-permute-start | bytes 4718600 | tf_op jit(solution)/shard_map/ppermute | solution.py:323
  1460.7 42.6 %collective-permute-start.6 = (bf16[1536,512]{1,0:T(8,128)(2,1)}, bf16[1536,512]{1,0:T(8,128)(2,1)S(1)}, u32[]{:S(2)}, u32[]{:S(2)}) collective-permute-start(bf16[1536,512]{1,0:T(8,128)(2,1)} %collective-permute-done.5), channel_id=1, source_target_pairs={{0,28},{4,0},{8,4},{12,8},{16,12},{20,16},{24,20},{28,24},{1,29},{... | collective-permute-start | bytes 4718600 | tf_op jit(solution)/shard_map/ppermute | solution.py:327
  (57 other events, 1887.1 us)
Sparse Core Ops, SparseCore 0:
  10.2 178.8 all-gather.17
  191.2 174.2 all-gather.7
  367.1 59.9 all-gather.9
  445.2 31.5 all-gather.11
  478.2 39.7 all-gather.15
  552.7 23.1 all-reduce.7
  577.5 71.1 all-gather.13
  678.9 23.3 all-reduce.9
  911.2 23.6 all-reduce.11
  937.0 219.7 reduce-scatter.4
  1159.1 244.8 reduce-scatter.8
  1406.1 210.3 all-gather.19
  1619.3 79.5 reduce-scatter.6
  1701.7 122.0 reduce-scatter.10
